TPU v7x, 128 devices: a whole 4x4x4 slice. The times are simulated.
128 devices in a mesh: req: 16 (over z, x_hi, core), mdl: 8 (over x_lo, y).
Axes of the slice: x: 4 (x_hi: 2, x_lo: 2; x = x_hi * 2 + x_lo), y: 4, z: 4, core: 2. Of those that a mesh axis runs over, the one named last changes fastest.
Arguments:
- tokens: bfloat16 [16384, 2048], P('req'), may hold values from -6 to 6
- doc_ids: int32 [16384], P('req'), may hold values from 0 to 16383, as said below
- positions: int32 [16384], P('req'), may hold values from 0 to 1023, as said below
- attn_gain: float32 [2048], replicated, may hold values from 0.5 to 1.5
- mlp_gain: float32 [2048], replicated, may hold values from 0.5 to 1.5
- q_gain: float32 [128], replicated, may hold values from 0.5 to 48
- key_norm_gain: float32 [128], replicated, may hold values from 0.5 to 1.5
- q_weight: float32 [2048, 2048], P('req', 'mdl'), may hold values from -0.125 to 0.125
- key_matrix: float32 [2048, 1024], P('req', 'mdl'), may hold values from -0.125 to 0.125
- value_matrix: float32 [2048, 1024], P('req', 'mdl'), may hold values from -0.125 to 0.125
- o_weight: float32 [2048, 2048], P('mdl', 'req'), may hold values from -0.125 to 0.125
- gate_weight: float32 [2048, 6144], P('mdl', 'req'), may hold values from -0.125 to 0.125
- up_weight: float32 [2048, 6144], P('mdl', 'req'), may hold values from -0.125 to 0.125
- down_weight: float32 [6144, 2048], P('req', 'mdl'), may hold values from -0.078125 to 0.078125
Outputs:
- layer_out: bfloat16 [16384, 2048], P(('req', 'mdl'))
- key_value_cache: bfloat16 [2, 16384, 1024], P(None, 'req', 'mdl')
Inputs may be any that keep to these rules, and one draw needn't show every extreme that they name: `doc_ids`: A row's prompt number is the index of its prompt's first row among all packed rows, so it never falls along the rows; a prompt holds at most 1024 rows, every aligned block of 1024 rows has a prompt start in its second half, every block but the first begins inside the prompt that the block before it ends with, and the last row starts a prompt. `positions`: positions count from 0 at each prompt's first row.
All inputs are finite; a program needn't handle non-finite values.
Results may differ from a plain program's by a relative error of at most 0.02.
The roundings to bfloat16 on the way count: a program that leaves them out, or rounds other values in their place, can miss the bound.
Values may be sent and summed in bfloat16 or wider, within the bound.
No kernel may reach another device: no remote copies, remote signals or barrier semaphores. Data moves between devices by JAX's collectives and lax.ppermute only.
A program may use at most 128 MiB of HBM per device.

v0:
```python
import math
import jax
import jax.numpy as jnp
from jax import lax
from jax.sharding import PartitionSpec as P

HEAD_SIZE = 128


def passed_along(block, axis, distance):
    devices = range(lax.axis_size(axis))
    route = [(i - distance, i) for i in devices if i - distance in devices]
    return lax.ppermute(block, axis, route)


def root_mean_scale(values, gain):
    return values * lax.rsqrt(jnp.mean(values * values, axis=-1, keepdims=True) + 1e-06) * gain


def apply_rotary(tensor, position):
    half = tensor.shape[-1] // 2
    freq = jnp.exp(
        jnp.arange(half, dtype=jnp.float32) * (-2.0 * math.log(1000000.0) / tensor.shape[-1])
    )
    angle = position.astype(jnp.float32)[:, None] * freq[None, :]
    cosine = jnp.cos(angle)[:, None, :]
    sine = jnp.sin(angle)[:, None, :]
    front = tensor[..., :half]
    back = tensor[..., half:]
    return jnp.concatenate([front * cosine - back * sine, back * cosine + front * sine], axis=-1)


def per_device(
    tokens,
    doc_ids,
    positions,
    attn_gain,
    mlp_gain,
    q_gain,
    key_norm_gain,
    q_weight,
    key_matrix,
    value_matrix,
    o_weight,
    gate_weight,
    up_weight,
    down_weight,
):
    rows_here = tokens.shape[0]
    normed = root_mean_scale(tokens.astype(jnp.float32), attn_gain).astype(jnp.bfloat16)
    query_cols = q_weight.shape[1]
    kv_cols = key_matrix.shape[1]
    pieces = (
        lax.all_gather(q_weight.astype(jnp.bfloat16), "req", axis=0, tiled=True),
        lax.all_gather(key_matrix.astype(jnp.bfloat16), "req", axis=0, tiled=True),
        lax.all_gather(value_matrix.astype(jnp.bfloat16), "req", axis=0, tiled=True),
    )
    query_raw, unnormed_keys, unnormed_values = tuple(
        (jnp.dot(normed, piece, preferred_element_type=jnp.float32) for piece in pieces)
    )
    q_heads = query_cols // HEAD_SIZE
    kv_heads = kv_cols // HEAD_SIZE
    head_groups = q_heads // kv_heads
    query_rows = apply_rotary(
        root_mean_scale(query_raw.reshape(rows_here, q_heads, HEAD_SIZE), q_gain), positions
    ).astype(jnp.bfloat16)
    rotated_keys = (
        apply_rotary(
            root_mean_scale(unnormed_keys.reshape(rows_here, kv_heads, HEAD_SIZE), key_norm_gain),
            positions,
        )
        .astype(jnp.bfloat16)
        .reshape(rows_here, kv_cols)
    )
    projected_values = unnormed_values.astype(jnp.bfloat16)
    key_value_cache = jnp.stack([rotated_keys, projected_values])
    prior_keys, prior_values = passed_along((rotated_keys, projected_values), "req", 1)
    all_keys = jnp.concatenate([prior_keys, rotated_keys], axis=0).reshape(-1, kv_heads, HEAD_SIZE)
    all_values = jnp.concatenate([prior_values, projected_values], axis=0).reshape(
        -1, kv_heads, HEAD_SIZE
    )
    prior_index = jnp.arange(prior_keys.shape[0], dtype=jnp.int32)
    prior_live = prior_index >= rows_here - positions[0]
    grouped_queries = query_rows.reshape(rows_here, kv_heads, head_groups, HEAD_SIZE)
    block_rows = min(512, rows_here)
    scale = HEAD_SIZE ** (-0.5)
    outputs = []
    for block_index in range(rows_here // block_rows):
        lower = block_index * block_rows
        block_q = grouped_queries[lower : lower + block_rows]
        block_doc = doc_ids[lower : lower + block_rows]
        block_pos = positions[lower : lower + block_rows]
        scores = (
            jnp.einsum("qkrd,skd->krqs", block_q, all_keys, preferred_element_type=jnp.float32)
            * scale
        )
        earlier = (block_doc == doc_ids[0])[:, None] & prior_live[None, :]
        current = (doc_ids[None, :] == block_doc[:, None]) & (
            positions[None, :] <= block_pos[:, None]
        )
        allowed = jnp.concatenate([earlier, current], axis=1)
        scores = jnp.where(allowed[None, None], scores, -jnp.inf)
        top = jnp.max(scores, axis=-1, keepdims=True)
        expo = jnp.exp(scores - top)
        probs = (expo / jnp.sum(expo, axis=-1, keepdims=True)).astype(jnp.bfloat16)
        context_block = jnp.einsum(
            "krqs,skd->qkrd", probs, all_values, preferred_element_type=jnp.float32
        )
        outputs.append(context_block.astype(jnp.bfloat16).reshape(block_rows, q_heads * HEAD_SIZE))
    context = jnp.concatenate(outputs, axis=0)
    head_terms = jnp.dot(
        context,
        lax.all_gather(o_weight.astype(jnp.bfloat16), "req", axis=1, tiled=True),
        preferred_element_type=jnp.float32,
    )
    attn_rows = lax.psum_scatter(
        head_terms.astype(jnp.bfloat16), "mdl", scatter_dimension=0, tiled=True
    ).astype(jnp.float32)
    share = rows_here // lax.axis_size("mdl")
    own_rows = lax.dynamic_slice_in_dim(tokens, lax.axis_index("mdl") * share, share, 0)
    resid = lax.optimization_barrier(
        (own_rows.astype(jnp.float32) + attn_rows).astype(jnp.bfloat16)
    ).astype(jnp.float32)
    mlp_in = root_mean_scale(resid, mlp_gain).astype(jnp.bfloat16)
    gate_local = gate_weight.astype(jnp.bfloat16)
    up_local = up_weight.astype(jnp.bfloat16)
    down_local = down_weight.astype(jnp.bfloat16)
    gate_whole, up_whole = (
        lax.all_gather(gate_local, "req", axis=1, tiled=True),
        lax.all_gather(up_local, "req", axis=1, tiled=True),
    )
    down_whole = lax.all_gather(down_local, "req", axis=0, tiled=True)
    gate_server, up_server = (
        lax.all_to_all(gate_whole, "mdl", split_axis=1, concat_axis=0, tiled=True),
        lax.all_to_all(up_whole, "mdl", split_axis=1, concat_axis=0, tiled=True),
    )
    down_server = lax.all_to_all(down_whole, "mdl", split_axis=0, concat_axis=1, tiled=True)
    piece = lax.all_gather(mlp_in, "mdl", axis=0, tiled=True)
    gate = jnp.dot(piece, gate_server, preferred_element_type=jnp.float32)
    upper = jnp.dot(piece, up_server, preferred_element_type=jnp.float32)
    hidden = (jax.nn.silu(gate) * upper).astype(jnp.bfloat16)
    unit_terms = jnp.dot(hidden, down_server, preferred_element_type=jnp.float32)
    mlp_rows = lax.psum_scatter(
        unit_terms.astype(jnp.bfloat16), "mdl", scatter_dimension=0, tiled=True
    ).astype(jnp.float32)
    layer_out = (resid + mlp_rows).astype(jnp.bfloat16)
    return (layer_out, key_value_cache)


def solution(mesh):
    in_specs = (
        P("req", None),
        P("req"),
        P("req"),
        P(),
        P(),
        P(),
        P(),
        P("req", "mdl"),
        P("req", "mdl"),
        P("req", "mdl"),
        P("mdl", "req"),
        P("mdl", "req"),
        P("mdl", "req"),
        P("req", "mdl"),
    )
    out_specs = (P(("req", "mdl"), None), P(None, "req", "mdl"))
    return jax.shard_map(
        per_device, mesh=mesh, in_specs=in_specs, out_specs=out_specs, check_vma=False
    )
```

profile of v0, /device:TPU:1, one launch (start us, length us, event | category | flops | bytes accessed | tf_op | source)
XLA Modules:
  0.0 521.2 jit_solution(16136902884525856238)
XLA Ops:
  10.5 3.2 fusion
  15.0 30.4 %all_gather.25 = bf16[2048,128]{1,0:T(8,128)(2,1)S(1)} all-gather(bf16[128,128]{1,0:T(8,128)(2,1)S(1)} %convert_element_type.105), channel_id=1, replica_groups=mesh['req'=16,'mdl'=8] {'req'}, dimensions={0}, use_global_device_ids=true | all-gather | bytes 557056 | tf_op jit(solution)/shard_map/all_gather | solution.py:55
  53.3 23.4 %all_gather.24 = bf16[2048,128]{1,0:T(8,128)(2,1)S(1)} all-gather(bf16[128,128]{1,0:T(8,128)(2,1)S(1)} %convert_element_type.103), channel_id=1, replica_groups=mesh['req'=16,'mdl'=8] {'req'}, dimensions={0}, use_global_device_ids=true | all-gather | bytes 557056 | tf_op jit(solution)/shard_map/all_gather | solution.py:56
  76.7 4.1 convolution_convert_fusion.2
  80.9 3.5 collective-permute-start
  93.3 4.8 multiply_reduce_fusion
  111.8 3.9 fusion.11
  115.7 3.9 fusion.14
  119.7 4.5 convolution_convert_fusion
  125.9 31.1 %all-gather.13.cloned.1.call-done = bf16[256,6144]{0,1:T(8,128)(2,1)} async-done(((bf16[256,384]{0,1:T(8,128)(2,1)}), bf16[256,6144]{0,1:T(8,128)(2,1)}) %all-gather.13.cloned.1.call-update) | async-done | bytes 3145744 | tf_op jit(solution)/shard_map/all_gather | solution.py:129
  157.0 4.1 all-to-all-start
  161.2 81.4 %reduce-scatter.3.cloned.1.call-done = bf16[128,2048]{1,0:T(8,128)(2,1)} async-done(((bf16[1024,2048]{1,0:T(8,128)(2,1)}), bf16[128,2048]{1,0:T(8,128)(2,1)}) %reduce-scatter.3.cloned.1.call-update) | async-done | bytes 524304 | tf_op jit(solution)/shard_map/reduce_scatter | solution.py:116
  245.7 49.2 %all-gather.15.cloned.1.call-done = bf16[256,6144]{0,1:T(8,128)(2,1)} async-done(((bf16[256,384]{0,1:T(8,128)(2,1)}), bf16[256,6144]{0,1:T(8,128)(2,1)}) %all-gather.15.cloned.1.call-update) | async-done | bytes 3145744 | tf_op jit(solution)/shard_map/all_gather | solution.py:130
  295.0 4.5 all-to-all-start.1
  299.5 54.8 %all-gather.17.cloned.1.call-done = bf16[6144,256]{1,0:T(8,128)(2,1)} async-done(((bf16[384,256]{1,0:T(8,128)(2,1)}), bf16[6144,256]{1,0:T(8,128)(2,1)}) %all-gather.17.cloned.1.call-update) | async-done | bytes 3145744 | tf_op jit(solution)/shard_map/all_gather | solution.py:132
  354.2 4.6 all-to-all-start.2
  358.9 3.1 copy.35
  362.0 3.3 copy.37
  365.2 54.4 %all-to-all-done.2 = bf16[8,768,256]{2,1,0:T(8,128)(2,1)} async-done(((bf16[8,768,256]{2,1,0:T(8,128)(2,1)}), bf16[8,768,256]{2,1,0:T(8,128)(2,1)}, u32[]{:S(2)}, u32[]{:S(2)}) %all-to-all-start.2) | async-done | bytes 3145760 | tf_op jit(solution)/shard_map/all_to_all | solution.py:137
  419.6 4.7 copy.38
  424.3 15.7 %all-gather.11.cloned.1.call-done = bf16[1024,2048]{1,0:T(8,128)(2,1)} async-done(((bf16[128,2048]{1,0:T(8,128)(2,1)}), bf16[1024,2048]{1,0:T(8,128)(2,1)}) %all-gather.11.cloned.1.call-update) | async-done | bytes 4194320 | tf_op jit(solution)/shard_map/all_gather | solution.py:138
  440.0 8.2 %fusion.49 = f32[1024,768]{1,0:T(8,128)} fusion(bf16[1024,2048]{1,0:T(8,128)(2,1)} %all-gather.11.cloned.1.call-done, bf16[2048,768]{1,0:T(8,128)(2,1)} %bitcast.100), kind=kOutput, calls=%fused_computation.91 | convolution fusion | flops 3221225472 | bytes 10485760 | tf_op jit(solution)/shard_map/dot_general | solution.py:139
  448.2 12.2 %convolution_convert_fusion.1 = bf16[1024,2048]{1,0:T(8,128)(2,1)} fusion(bf16[768,2048]{0,1:T(8,128)(2,1)} %bitcast.101, f32[1024,768]{1,0:T(8,128)} %fusion.49, bf16[1024,2048]{1,0:T(8,128)(2,1)} %all-gather.11.cloned.1.call-done, bf16[2048,768]{1,0:T(8,128)(2,1)S(1)} %bitcast.99), kind=kOutput, calls=%fused_computation.22 | convolution fusion | flops 6449266688 | bytes 17825792 | tf_op jit(solution)/shard_map/dot_general | solution.py:142
  463.3 49.1 %reduce-scatter.5.cloned.1.call-done = bf16[128,2048]{1,0:T(8,128)(2,1)} async-done(((bf16[1024,2048]{1,0:T(8,128)(2,1)}), bf16[128,2048]{1,0:T(8,128)(2,1)}) %reduce-scatter.5.cloned.1.call-update) | async-done | bytes 524304 | tf_op jit(solution)/shard_map/reduce_scatter | solution.py:143
  (100 shorter events, 43.8 us)
Async XLA Ops:
  7.2 6.5 %copy-start.10 = (f32[128,128]{1,0:T(8,128)S(1)}, f32[128,128]{1,0:T(8,128)}, u32[]{:S(2)}) copy-start(f32[128,128]{1,0:T(8,128)} %param.22) | copy-start | bytes 196612
  7.2 6.6 %copy-start.14 = (f32[2048]{0:T(1024)S(1)}, f32[2048]{0:T(1024)}, u32[]{:S(2)}) copy-start(f32[2048]{0:T(1024)} %param.17) | copy-start | bytes 24580
  7.2 86.1 %all-gather.7.cloned.1.call-start = ((), (), s32[]{:S(2)}) async-start(), calls=%async_computation.5 | async-start | bytes 1114112 | tf_op jit(solution)/shard_map/all_gather | solution.py:54
  8.8 110.9 %all-gather.9.cloned.1.call-start = ((), (), s32[]{:S(2)}) async-start(), calls=%async_computation.6 | async-start | bytes 1114112 | tf_op jit(solution)/shard_map/all_gather | solution.py:113
  10.4 146.6 %all-gather.13.cloned.1.call-start = ((), (), s32[]{:S(2)}) async-start(), calls=%async_computation.9 | async-start | bytes 3342336 | tf_op jit(solution)/shard_map/all_gather | solution.py:129
  14.9 30.5 %copy-start.1 = (bf16[1024,2048]{1,0:T(8,128)(2,1)}, bf16[1024,2048]{1,0:T(8,128)(2,1)S(1)}, u32[]{:S(2)}) copy-start(bf16[1024,2048]{1,0:T(8,128)(2,1)S(1)} %fusion.2) | copy-start | bytes 12582916
  14.9 32.2 %copy-start.12 = (s32[1024]{0:T(1024)S(1)}, s32[1024]{0:T(1024)}, u32[]{:S(2)}) copy-start(s32[1024]{0:T(1024)} %param.16) | copy-start | bytes 12292
  15.0 32.2 %copy-start.16 = (f32[128]{0:T(128)S(1)}, f32[128]{0:T(128)}, u32[]{:S(2)}) copy-start(f32[128]{0:T(128)} %param.20) | copy-start | bytes 1540
  45.4 7.9 %copy-start.11 = (f32[128,128]{1,0:T(8,128)S(1)}, f32[128,128]{1,0:T(8,128)}, u32[]{:S(2)}) copy-start(f32[128,128]{1,0:T(8,128)} %param.23) | copy-start | bytes 196612
  49.8 34.6 %copy-start.7 = (f32[256,384]{1,0:T(8,128)S(1)}, f32[256,384]{1,0:T(8,128)}, u32[]{:S(2)}) copy-start(f32[256,384]{1,0:T(8,128)} %param.25) | copy-start | bytes 1179652
  50.5 35.0 %copy-start.13 = (s32[1024]{0:T(1024)S(1)}, s32[1024]{0:T(1024)}, u32[]{:S(2)}) copy-start(s32[1024]{0:T(1024)} %param.15) | copy-start | bytes 12292
  51.4 50.4 %collective-permute-start.1 = (bf16[1024,128]{1,0:T(8,128)(2,1)}, bf16[1024,128]{1,0:T(8,128)(2,1)}, u32[]{:S(2)}, u32[]{:S(2)}) collective-permute-start(bf16[1024,128]{1,0:T(8,128)(2,1)} %pad_maximum_fusion.3), channel_id=1, source_target_pairs={{0,8},{8,16},{16,24},{24,32},{32,40},{40,48},{48,56},{56,64},{64,7... | collective-permute-start | bytes 786440 | tf_op jit(solution)/shard_map/ppermute | solution.py:13
  80.9 31.0 %collective-permute-start = (bf16[1024,128]{1,0:T(8,128)(2,1)}, bf16[1024,128]{1,0:T(8,128)(2,1)}, u32[]{:S(2)}, u32[]{:S(2)}) collective-permute-start(bf16[1024,128]{1,0:T(8,128)(2,1)} %convolution_convert_fusion.2), channel_id=1, source_target_pairs={{0,8},{8,16},{16,24},{24,32},{32,40},{40,48},{48,56},{56,64},{64,7... | collective-permute-start | bytes 786440 | tf_op jit(solution)/shard_map/ppermute | solution.py:13
  85.2 157.4 %reduce-scatter.3.cloned.1.call-start = ((), (), s32[]{:S(2)}) async-start(), calls=%async_computation.7 | async-start | bytes 4718592 | tf_op jit(solution)/shard_map/reduce_scatter | solution.py:116
  93.3 6.5 %copy-start.17 = (f32[128]{0:T(128)S(1)}, f32[128]{0:T(128)}, u32[]{:S(2)}) copy-start(f32[128]{0:T(128)} %param.19) | copy-start | bytes 1540
  124.2 170.8 %all-gather.15.cloned.1.call-start = ((), (), s32[]{:S(2)}) async-start(), calls=%async_computation.10 | async-start | bytes 3342336 | tf_op jit(solution)/shard_map/all_gather | solution.py:130
  125.1 229.1 %all-gather.17.cloned.1.call-start = ((), (), s32[]{:S(2)}) async-start(), calls=%async_computation.11 | async-start | bytes 3342336 | tf_op jit(solution)/shard_map/all_gather | solution.py:132
  157.0 87.7 %copy-start.15 = (f32[2048]{0:T(1024)S(1)}, f32[2048]{0:T(1024)}, u32[]{:S(2)}) copy-start(f32[2048]{0:T(1024)} %param.18) | copy-start | bytes 24580
  157.0 138.0 %all-to-all-start = ((bf16[256,8,768]{0,2,1:T(8,128)(2,1)}), bf16[256,8,768]{0,2,1:T(8,128)(2,1)S(1)}, u32[]{:S(2)}, u32[]{:S(2)}) async-start(bf16[256,8,768]{0,2,1:T(8,128)(2,1)} %bitcast.96), calls=%async_computation.1 | async-start | bytes 6291456 | tf_op jit(solution)/shard_map/all_to_all | solution.py:134
  161.2 278.8 %all-gather.11.cloned.1.call-start = ((), (), s32[]{:S(2)}) async-start(), calls=%async_computation.8 | async-start | bytes 4718592 | tf_op jit(solution)/shard_map/all_gather | solution.py:138
  295.0 59.3 %all-to-all-start.1 = ((bf16[256,8,768]{0,2,1:T(8,128)(2,1)}), bf16[256,8,768]{0,2,1:T(8,128)(2,1)}, u32[]{:S(2)}, u32[]{:S(2)}) async-start(bf16[256,8,768]{0,2,1:T(8,128)(2,1)} %bitcast.98), calls=%async_computation.2 | async-start | bytes 6291456 | tf_op jit(solution)/shard_map/all_to_all | solution.py:135
  354.2 65.3 %all-to-all-start.2 = ((bf16[8,768,256]{2,1,0:T(8,128)(2,1)}), bf16[8,768,256]{2,1,0:T(8,128)(2,1)}, u32[]{:S(2)}, u32[]{:S(2)}) async-start(bf16[8,768,256]{2,1,0:T(8,128)(2,1)} %bitcast.97), calls=%async_computation.3 | async-start | bytes 6291456 | tf_op jit(solution)/shard_map/all_to_all | solution.py:137
  358.8 153.6 %reduce-scatter.5.cloned.1.call-start = ((), (), s32[]{:S(2)}) async-start(), calls=%async_computation.12 | async-start | bytes 4718592 | tf_op jit(solution)/shard_map/reduce_scatter | solution.py:143
  460.4 52.0 %copy-start.3 = (bf16[128,2048]{1,0:T(8,128)(2,1)S(1)}, bf16[128,2048]{1,0:T(8,128)(2,1)}, u32[]{:S(2)}) copy-start(bf16[128,2048]{1,0:T(8,128)(2,1)} %copy-done.2) | copy-start | bytes 1572868
  (7 other events, 13.6 us)
Sparse Core Ops, SparseCore 0:
  10.5 48.5 all-gather.6
  61.5 42.2 all-gather.8
  106.2 50.8 all-gather.12
  159.3 83.2 reduce-scatter.2
  244.9 50.0 all-gather.14
  297.3 56.8 all-gather.16
  356.5 83.5 all-gather.10
  460.6 51.7 reduce-scatter.4
where the time goes:
time: 522 us; the launch traced here: 521 us
  waiting for transfers between devices  336 us (64%)
  blocking collectives  53.9 us (10%)
  matrix products  49.1 us (9%)
  other arithmetic  30.2 us (6%)
  starting transfers between devices  19.1 us (4%)
  local copies, waits for them, and re-layouts  17.9 us (3%)
  between operations  15.1 us (3%)
    reduce_scatter x1, waiting for transfers between devices, per_device(): lax.psum_scatter(head_terms.astype(jnp.bfloat16), 'mdl', scatter_dimensio...  81.4 us
    all_gather x1, waiting for transfers between devices, per_device(): down_whole = lax.all_gather(down_local, 'req', axis=0, tiled=True)  54.8 us
    all_to_all x1, waiting for transfers between devices, per_device(): lax.all_to_all(down_whole, 'mdl', split_axis=0, concat_axis=1, tiled=True)  54.4 us
    all_gather x1, waiting for transfers between devices, per_device(): lax.all_gather(up_local, 'req', axis=1, tiled=True)  49.2 us
    reduce_scatter x1, waiting for transfers between devices, per_device(): lax.psum_scatter(unit_terms.astype(jnp.bfloat16), 'mdl', scatter_dimensio...  49.1 us
    all_gather x1, waiting for transfers between devices, per_device(): lax.all_gather(gate_local, 'req', axis=1, tiled=True)  31.1 us
    all_gather x1, blocking collectives, per_device(): lax.all_gather(key_matrix.astype(jnp.bfloat16), 'req', axis=0, tiled=True)  30.4 us
    all_gather x1, blocking collectives, per_device(): lax.all_gather(value_matrix.astype(jnp.bfloat16), 'req', axis=0, tiled=True)  23.4 us
  transfers between devices with their start and end apart: 13, of which 7 were waited for; matrix products, arithmetic and copies ran while one was open for 14% of the time, Pallas kernels for 0%

commit v1 on v0

--- a/solution.py
+++ b/solution.py
@@ -135,7 +135,9 @@
         lax.all_to_all(up_whole, "mdl", split_axis=1, concat_axis=0, tiled=True),
     )
     down_server = lax.all_to_all(down_whole, "mdl", split_axis=0, concat_axis=1, tiled=True)
-    piece = lax.all_gather(mlp_in, "mdl", axis=0, tiled=True)
+    field_out = jnp.stack([mlp_in for _ in range(lax.axis_size("mdl"))], axis=0)
+    shaped = lax.all_to_all(field_out, "mdl", split_axis=0, concat_axis=0)
+    piece = jnp.concatenate(shaped, axis=0)
     gate = jnp.dot(piece, gate_server, preferred_element_type=jnp.float32)
     upper = jnp.dot(piece, up_server, preferred_element_type=jnp.float32)
     hidden = (jax.nn.silu(gate) * upper).astype(jnp.bfloat16)

time: 522 us -> 503 us (0.964)
  waiting for transfers between devices: 336 us -> 305 us
  local copies, waits for them, and re-layouts: 17.9 us -> 25.1 us
    all_to_all x1, waiting for transfers between devices: 54.4 us -> 0.01 us  [per_device(): lax.all_to_all(down_whole, 'mdl', split_axis=0, concat_axis=1, tiled=True)]
    all_to_all x0 -> x1, waiting for transfers between devices: none -> 37.7 us  [per_device(): shaped = lax.all_to_all(field_out, 'mdl', split_axis=0, concat_axis=0)]
    all_gather x1 -> x0, waiting for transfers between devices: 15.7 us -> none  [per_device(): piece = lax.all_gather(mlp_in, 'mdl', axis=0, tiled=True)]
    all_gather x1, waiting for transfers between devices: 49.2 us -> 55.2 us  [per_device(): lax.all_gather(up_local, 'req', axis=1, tiled=True)]
  transfers between devices with their start and end apart: 13 -> 13, of which waited for: 7 -> 6; matrix products, arithmetic and copies ran while one was open for 14% -> 15% of each run, Pallas kernels for 0% -> 0%
where the time goes in v1:
time: 503 us; the launch traced here: 502 us
  waiting for transfers between devices  305 us (61%)
  blocking collectives  52.5 us (10%)
  matrix products  49.1 us (10%)
  other arithmetic  31.3 us (6%)
  local copies, waits for them, and re-layouts  25.1 us (5%)
  starting transfers between devices  24 us (5%)
  between operations  15.1 us (3%)
    reduce_scatter x1, waiting for transfers between devices, per_device(): lax.psum_scatter(head_terms.astype(jnp.bfloat16), 'mdl', scatter_dimensio...  81.3 us
    all_gather x1, waiting for transfers between devices, per_device(): lax.all_gather(up_local, 'req', axis=1, tiled=True)  55.2 us
    all_gather x1, waiting for transfers between devices, per_device(): down_whole = lax.all_gather(down_local, 'req', axis=0, tiled=True)  55.1 us
    reduce_scatter x1, waiting for transfers between devices, per_device(): lax.psum_scatter(unit_terms.astype(jnp.bfloat16), 'mdl', scatter_dimensio...  48.7 us
    all_to_all x1, waiting for transfers between devices, per_device(): shaped = lax.all_to_all(field_out, 'mdl', split_axis=0, concat_axis=0)  37.7 us
    all_gather x1, blocking collectives, per_device(): lax.all_gather(key_matrix.astype(jnp.bfloat16), 'req', axis=0, tiled=True)  29.1 us
    all_gather x1, waiting for transfers between devices, per_device(): lax.all_gather(gate_local, 'req', axis=1, tiled=True)  26.8 us
    all_gather x1, blocking collectives, per_device(): lax.all_gather(value_matrix.astype(jnp.bfloat16), 'req', axis=0, tiled=True)  23.3 us
  transfers between devices with their start and end apart: 13, of which 6 were waited for; matrix products, arithmetic and copies ran while one was open for 15% of the time, Pallas kernels for 0%

profile of v1, /device:TPU:1, one launch (start us, length us, event | category | flops | bytes accessed | tf_op | source)
XLA Modules:
  0.0 502.0 jit_solution(10709741918445854309)
XLA Ops:
  15.2 3.3 fusion
  18.6 29.1 %all_gather.22 = bf16[2048,128]{1,0:T(8,128)(2,1)S(1)} all-gather(bf16[128,128]{1,0:T(8,128)(2,1)S(1)} %convert_element_type.105), channel_id=1, replica_groups=mesh['req'=16,'mdl'=8] {'req'}, dimensions={0}, use_global_device_ids=true | all-gather | bytes 557056 | tf_op jit(solution)/shard_map/all_gather | solution.py:55
  58.6 23.3 %all_gather.21 = bf16[2048,128]{1,0:T(8,128)(2,1)S(1)} all-gather(bf16[128,128]{1,0:T(8,128)(2,1)S(1)} %convert_element_type.103), channel_id=1, replica_groups=mesh['req'=16,'mdl'=8] {'req'}, dimensions={0}, use_global_device_ids=true | all-gather | bytes 557056 | tf_op jit(solution)/shard_map/all_gather | solution.py:56
  81.9 4.1 convolution_convert_fusion.2
  86.1 3.7 collective-permute-start
  98.8 4.8 multiply_reduce_fusion
  117.2 3.9 fusion.11
  121.1 3.9 fusion.14
  125.1 4.5 convolution_convert_fusion
  129.6 26.8 %all-gather.10.cloned.1.call-done = bf16[256,6144]{0,1:T(8,128)(2,1)} async-done(((bf16[256,384]{0,1:T(8,128)(2,1)}), bf16[256,6144]{0,1:T(8,128)(2,1)}) %all-gather.10.cloned.1.call-update) | async-done | bytes 3145744 | tf_op jit(solution)/shard_map/all_gather | solution.py:129
  156.4 4.0 all-to-all-start.1
  160.4 55.2 %all-gather.12.cloned.1.call-done = bf16[256,6144]{0,1:T(8,128)(2,1)} async-done(((bf16[256,384]{0,1:T(8,128)(2,1)}), bf16[256,6144]{0,1:T(8,128)(2,1)}) %all-gather.12.cloned.1.call-update) | async-done | bytes 3145744 | tf_op jit(solution)/shard_map/all_gather | solution.py:130
  215.6 4.6 all-to-all-start.2
  220.2 55.1 %all-gather.14.cloned.1.call-done = bf16[6144,256]{1,0:T(8,128)(2,1)} async-done(((bf16[384,256]{1,0:T(8,128)(2,1)}), bf16[6144,256]{1,0:T(8,128)(2,1)}) %all-gather.14.cloned.1.call-update) | async-done | bytes 3145744 | tf_op jit(solution)/shard_map/all_gather | solution.py:132
  275.3 4.7 all-to-all-start.3
  280.1 81.3 %reduce-scatter.3.cloned.1.call-done = bf16[128,2048]{1,0:T(8,128)(2,1)} async-done(((bf16[1024,2048]{1,0:T(8,128)(2,1)}), bf16[128,2048]{1,0:T(8,128)(2,1)}) %reduce-scatter.3.cloned.1.call-update) | async-done | bytes 524304 | tf_op jit(solution)/shard_map/reduce_scatter | solution.py:116
  364.5 3.5 stack.6
  368.0 4.6 all-to-all-start
  375.7 3.2 copy.37
  378.9 4.7 copy.38
  383.5 37.7 %all-to-all-done = bf16[8,128,2048]{2,1,0:T(8,128)(2,1)} async-done(((bf16[8,128,2048]{2,1,0:T(8,128)(2,1)}), bf16[8,128,2048]{2,1,0:T(8,128)(2,1)}, u32[]{:S(2)}, u32[]{:S(2)}) %all-to-all-start) | async-done | bytes 4194336 | tf_op jit(solution)/shard_map/all_to_all | solution.py:139
  421.2 8.2 %fusion.49 = f32[1024,768]{1,0:T(8,128)} fusion(bf16[1024,2048]{1,0:T(8,128)(2,1)} %bitcast.21, bf16[2048,768]{1,0:T(8,128)(2,1)} %bitcast.101), kind=kOutput, calls=%fused_computation.91 | convolution fusion | flops 3221225472 | bytes 10485760 | tf_op jit(solution)/shard_map/dot_general | solution.py:141
  429.4 12.3 %convolution_convert_fusion.1 = bf16[1024,2048]{1,0:T(8,128)(2,1)} fusion(bf16[768,2048]{0,1:T(8,128)(2,1)} %bitcast.102, f32[1024,768]{1,0:T(8,128)} %fusion.49, bf16[1024,2048]{1,0:T(8,128)(2,1)} %bitcast.21, bf16[2048,768]{1,0:T(8,128)(2,1)S(1)} %bitcast.100), kind=kOutput, calls=%fused_computation.22 | convolution fusion | flops 6449266688 | bytes 17825792 | tf_op jit(solution)/shard_map/dot_general | solution.py:144
  444.6 48.7 %reduce-scatter.5.cloned.1.call-done = bf16[128,2048]{1,0:T(8,128)(2,1)} async-done(((bf16[1024,2048]{1,0:T(8,128)(2,1)}), bf16[128,2048]{1,0:T(8,128)(2,1)}) %reduce-scatter.5.cloned.1.call-update) | async-done | bytes 524304 | tf_op jit(solution)/shard_map/reduce_scatter | solution.py:145
  (94 shorter events, 51.7 us)
Async XLA Ops:
  7.2 40.5 %copy-start.11 = (f32[2048]{0:T(1024)S(1)}, f32[2048]{0:T(1024)}, u32[]{:S(2)}) copy-start(f32[2048]{0:T(1024)} %param.17) | copy-start | bytes 24580
  7.2 91.6 %all-gather.6.cloned.1.call-start = ((), (), s32[]{:S(2)}) async-start(), calls=%async_computation.6 | async-start | bytes 1114112 | tf_op jit(solution)/shard_map/all_gather | solution.py:54
  8.8 116.3 %all-gather.8.cloned.1.call-start = ((), (), s32[]{:S(2)}) async-start(), calls=%async_computation.7 | async-start | bytes 1114112 | tf_op jit(solution)/shard_map/all_gather | solution.py:113
  10.4 146.0 %all-gather.10.cloned.1.call-start = ((), (), s32[]{:S(2)}) async-start(), calls=%async_computation.9 | async-start | bytes 3342336 | tf_op jit(solution)/shard_map/all_gather | solution.py:129
  12.3 203.4 %all-gather.12.cloned.1.call-start = ((), (), s32[]{:S(2)}) async-start(), calls=%async_computation.10 | async-start | bytes 3342336 | tf_op jit(solution)/shard_map/all_gather | solution.py:130
  14.2 261.1 %all-gather.14.cloned.1.call-start = ((), (), s32[]{:S(2)}) async-start(), calls=%async_computation.11 | async-start | bytes 3342336 | tf_op jit(solution)/shard_map/all_gather | solution.py:132
  14.2 33.5 %copy-start = (bf16[1024,2048]{1,0:T(8,128)(2,1)S(1)}, bf16[1024,2048]{1,0:T(8,128)(2,1)}, u32[]{:S(2)}) copy-start(bf16[1024,2048]{1,0:T(8,128)(2,1)} %param.14) | copy-start | bytes 12582916
  48.7 1.9 copy-start.1
  50.7 1.8 copy-start.13
  50.7 7.9 %copy-start.8 = (f32[128,128]{1,0:T(8,128)S(1)}, f32[128,128]{1,0:T(8,128)}, u32[]{:S(2)}) copy-start(f32[128,128]{1,0:T(8,128)} %param.23) | copy-start | bytes 196612
  55.1 34.7 %copy-start.7 = (f32[384,256]{1,0:T(8,128)S(1)}, f32[384,256]{1,0:T(8,128)}, u32[]{:S(2)}) copy-start(f32[384,256]{1,0:T(8,128)} %param.27) | copy-start | bytes 1179652
  55.8 35.0 %copy-start.10 = (s32[1024]{0:T(1024)S(1)}, s32[1024]{0:T(1024)}, u32[]{:S(2)}) copy-start(s32[1024]{0:T(1024)} %param.15) | copy-start | bytes 12292
  56.7 50.5 %collective-permute-start.1 = (bf16[1024,128]{1,0:T(8,128)(2,1)}, bf16[1024,128]{1,0:T(8,128)(2,1)}, u32[]{:S(2)}, u32[]{:S(2)}) collective-permute-start(bf16[1024,128]{1,0:T(8,128)(2,1)} %pad_maximum_fusion.3), channel_id=1, source_target_pairs={{0,8},{8,16},{16,24},{24,32},{32,40},{40,48},{48,56},{56,64},{64,7... | collective-permute-start | bytes 786440 | tf_op jit(solution)/shard_map/ppermute | solution.py:13
  86.1 31.2 %collective-permute-start = (bf16[1024,128]{1,0:T(8,128)(2,1)}, bf16[1024,128]{1,0:T(8,128)(2,1)}, u32[]{:S(2)}, u32[]{:S(2)}) collective-permute-start(bf16[1024,128]{1,0:T(8,128)(2,1)} %convolution_convert_fusion.2), channel_id=1, source_target_pairs={{0,8},{8,16},{16,24},{24,32},{32,40},{40,48},{48,56},{56,64},{64,7... | collective-permute-start | bytes 786440 | tf_op jit(solution)/shard_map/ppermute | solution.py:13
  90.5 270.8 %reduce-scatter.3.cloned.1.call-start = ((), (), s32[]{:S(2)}) async-start(), calls=%async_computation.8 | async-start | bytes 4718592 | tf_op jit(solution)/shard_map/reduce_scatter | solution.py:116
  98.7 6.4 %copy-start.14 = (f32[128]{0:T(128)S(1)}, f32[128]{0:T(128)}, u32[]{:S(2)}) copy-start(f32[128]{0:T(128)} %param.19) | copy-start | bytes 1540
  105.1 2.1 copy-start.5
  156.4 59.3 %all-to-all-start.1 = ((bf16[256,8,768]{0,2,1:T(8,128)(2,1)}), bf16[256,8,768]{0,2,1:T(8,128)(2,1)S(1)}, u32[]{:S(2)}, u32[]{:S(2)}) async-start(bf16[256,8,768]{0,2,1:T(8,128)(2,1)} %bitcast.98), calls=%async_computation.2 | async-start | bytes 6291456 | tf_op jit(solution)/shard_map/all_to_all | solution.py:134
  215.6 59.7 %all-to-all-start.2 = ((bf16[256,8,768]{0,2,1:T(8,128)(2,1)}), bf16[256,8,768]{0,2,1:T(8,128)(2,1)}, u32[]{:S(2)}, u32[]{:S(2)}) async-start(bf16[256,8,768]{0,2,1:T(8,128)(2,1)} %bitcast.97), calls=%async_computation.3 | async-start | bytes 6291456 | tf_op jit(solution)/shard_map/all_to_all | solution.py:135
  275.3 88.1 %copy-start.12 = (f32[2048]{0:T(1024)S(1)}, f32[2048]{0:T(1024)}, u32[]{:S(2)}) copy-start(f32[2048]{0:T(1024)} %param.18) | copy-start | bytes 24580
  275.3 89.1 %all-to-all-start.3 = ((bf16[8,768,256]{2,1,0:T(8,128)(2,1)}), bf16[8,768,256]{2,1,0:T(8,128)(2,1)}, u32[]{:S(2)}, u32[]{:S(2)}) async-start(bf16[8,768,256]{2,1,0:T(8,128)(2,1)} %bitcast.99), calls=%async_computation.4 | async-start | bytes 6291456 | tf_op jit(solution)/shard_map/all_to_all | solution.py:137
  368.0 53.2 %all-to-all-start = ((bf16[8,128,2048]{2,1,0:T(8,128)(2,1)}), bf16[8,128,2048]{2,1,0:T(8,128)(2,1)}, u32[]{:S(2)}, u32[]{:S(2)}) async-start(bf16[8,128,2048]{2,1,0:T(8,128)(2,1)} %stack.6), calls=%async_computation.1 | async-start | bytes 8388608 | tf_op jit(solution)/shard_map/all_to_all | solution.py:139
  372.6 120.7 %reduce-scatter.5.cloned.1.call-start = ((), (), s32[]{:S(2)}) async-start(), calls=%async_computation.12 | async-start | bytes 4718592 | tf_op jit(solution)/shard_map/reduce_scatter | solution.py:145
  441.7 51.5 %copy-start.3 = (bf16[128,2048]{1,0:T(8,128)(2,1)S(1)}, bf16[128,2048]{1,0:T(8,128)(2,1)}, u32[]{:S(2)}) copy-start(bf16[128,2048]{1,0:T(8,128)(2,1)} %copy-done.2) | copy-start | bytes 1572868
  (4 other events, 4.2 us)
Sparse Core Ops, SparseCore 0:
  10.5 48.5 all-gather.5
  61.5 41.5 all-gather.7
  105.6 50.7 all-gather.9
  158.7 56.8 all-gather.11
  217.9 57.3 all-gather.13
  277.6 83.7 reduce-scatter.2
  441.9 51.3 reduce-scatter.4
